TPU v7x, 32 devices: a whole 2x2x4 slice. The times are simulated.
32 devices in a mesh: row: 8 (over y, x, core), col: 4 (over z).
Axes of the slice: x: 2, y: 2, z: 4, core: 2. Of those that a mesh axis runs over, the one named last changes fastest.
Arguments:
- hessian: float32 [8, 2048, 16, 1024], P(None, 'row', None, 'col'), as said below
Outputs:
- factored: float32 [8, 2048, 16, 1024], P(None, 'row', None, 'col')
Inputs may be any that keep to these rules, and one draw needn't show every extreme that they name: hessian, read as the 16384 x 16384 matrix H0, is symmetric and positive definite.
All inputs are finite; a program needn't handle non-finite values.
Results may differ from a plain program's by a relative error of at most 0.0003.
Values sent between devices are 32-bit elements; how exact they have to be, the bound alone decides.
No kernel may reach another device: no remote copies, remote signals or barrier semaphores. Data moves between devices by JAX's collectives and lax.ppermute only.
A program may use at most 192 MiB of HBM per device.

v0:
```python
import jax
import jax.numpy as jnp
from jax import lax
from jax.sharding import PartitionSpec as P


def broadcast(x, axis, root):
    mine = lax.axis_index(axis) == root
    return lax.psum(jnp.where(mine, x, jnp.zeros_like(x)), axis)


def invert_factor(diagonal):
    lower_factor = jnp.linalg.cholesky(diagonal)
    identity = jnp.eye(diagonal.shape[0], dtype=diagonal.dtype)
    return lax.linalg.triangular_solve(lower_factor, identity, left_side=True, lower=True)


def outer_update(own_panel, across):
    row_cycles, block_width, depth = own_panel.shape
    column_count = across.shape[0]
    product_flat = jnp.dot(
        own_panel.reshape(row_cycles * block_width, depth),
        across.reshape(column_count * block_width, depth).T,
        precision=lax.Precision.HIGHEST,
    )
    return product_flat.reshape(row_cycles, block_width, column_count, block_width)


def on_device(hessian):
    row_count = lax.axis_size("row")
    column_count = lax.axis_size("col")
    row_index = lax.axis_index("row")
    column_index = lax.axis_index("col")
    row_cycles, block_width, column_cycles, _ = hessian.shape
    row_blocks = row_index + row_count * jnp.arange(row_cycles, dtype=jnp.int32)
    col_blocks = column_index + column_count * jnp.arange(column_cycles, dtype=jnp.int32)
    offsets = jnp.arange(block_width, dtype=jnp.int32)
    row_position = row_blocks[:, None] * block_width + offsets[None, :]

    def apply_factor(column, inverse, panel_index):
        own_panel = jnp.dot(
            column.reshape(row_cycles * block_width, block_width),
            inverse.T,
            precision=lax.Precision.HIGHEST,
        )
        own_panel = own_panel.reshape(row_cycles, block_width, block_width)
        keep_mask = row_position[:, :, None] >= panel_index * block_width + offsets[None, None, :]
        return jnp.where(keep_mask, own_panel, jnp.zeros_like(own_panel))

    matrix = hessian
    slabs = []
    for root_col in range(2):
        slabs.append(broadcast(matrix[:, :, 0, :], "col", root_col))
    leading = jnp.stack(slabs, axis=2)
    blocks = []
    for root_row in range(2):
        blocks.append(broadcast(leading[0], "row", root_row))
    upper_rows, lower_rows = blocks
    first_inverse = invert_factor(upper_rows[:, 0, :])
    lower_first = jnp.dot(lower_rows[:, 0, :], first_inverse.T, precision=lax.Precision.HIGHEST)
    second_diag = lower_rows[:, 1, :] - jnp.dot(
        lower_first, lower_first.T, precision=lax.Precision.HIGHEST
    )
    second_inverse = invert_factor(second_diag)
    first_panel = apply_factor(leading[:, :, 0, :], first_inverse, 0)
    first_flat = first_panel.reshape(row_cycles * block_width, block_width)
    second_column = leading[:, :, 1, :] - jnp.dot(
        first_flat, lower_first.T, precision=lax.Precision.HIGHEST
    ).reshape(row_cycles, block_width, block_width)
    second_panel = apply_factor(second_column, second_inverse, 1)
    both_panels = jnp.concatenate([first_panel, second_panel], axis=2)
    depth = both_panels.shape[2]
    pieces = []
    for root_half in range(2):
        pieces.append(broadcast(both_panels, "row", column_index + root_half * column_count))
    across = jnp.stack(pieces, axis=1)
    both_across = across.reshape(column_cycles, block_width, depth)
    matrix = matrix - outer_update(both_panels, both_across)
    row_global = row_blocks[:, None, None, None]
    col_global = col_blocks[None, None, :, None]
    result = jnp.where(row_global < 2, jnp.zeros_like(matrix), matrix)
    result = jnp.where(col_global == 0, first_panel[:, :, None, :], result)
    result = jnp.where(col_global == 1, second_panel[:, :, None, :], result)
    return result


def solution(mesh):
    in_specs = (P(None, "row", None, "col"),)
    out_specs = P(None, "row", None, "col")
    return jax.shard_map(
        on_device, mesh=mesh, in_specs=in_specs, out_specs=out_specs, check_vma=False
    )
```

profile of v0, /device:TPU:0, one launch (start us, length us, event | category | flops | bytes accessed | tf_op | source)
XLA Modules:
  0.0 689.8 jit_solution(3838025563756587711)
XLA Ops:
  6.5 8.3 %slice.55 = f32[8,256,1,256]{3,2,1,0:T(1,128)} slice(f32[8,256,16,256]{3,2,1,0:T(8,128)} %param.4), slice={[0:8], [0:256], [0:1], [0:256]} | slice | bytes 4194304 | tf_op jit(solution)/shard_map/slice | solution.py:53
  14.8 4.5 copy.33
  19.4 2.4 select_bitcast_fusion.3
  21.9 157.8 %all-reduce.12.cloned.1.call-done = (f32[8,256,256]{1,2,0:T(8,128)}, f32[8,256,256]{1,2,0:T(8,128)}) async-done(((f32[8,256,256]{1,2,0:T(8,128)}, f32[8,256,256]{1,2,0:T(8,128)}), (f32[8,256,256]{1,2,0:T(8,128)}, f32[8,256,256]{1,2,0:T(8,128)})) %all-reduce.12.cloned.1.call-update) | async-done | bytes 4194320 | tf_op jit(solution)/shard_map/psum | solution.py:9
  179.7 1.9 select_bitcast_fusion.4
  182.6 56.1 %all-reduce.10.cloned.1.call-done = (f32[256,2,256]{0,2,1:T(8,128)}, f32[256,2,256]{0,2,1:T(8,128)}) async-done(((f32[256,2,256]{0,2,1:T(8,128)}, f32[256,2,256]{0,2,1:T(8,128)}), (f32[256,2,256]{0,2,1:T(8,128)}, f32[256,2,256]{0,2,1:T(8,128)})) %all-reduce.10.cloned.1.call-update) | async-done | bytes 1048592 | tf_op jit(solution)/shard_map/psum | solution.py:9
  239.8 1.0 fusion.12
  240.8 11.7 %cholesky.130 = f32[128,128]{1,0:T(8,128)S(1)} custom-call(f32[128,128]{1,0:T(8,128)S(1)} %cholesky.194), custom_call_target="Cholesky" | custom-call | tf_op jit(solution)/shard_map/jit(cholesky)/cholesky | solution.py:13
  252.5 9.8 %custom-call.13 = f32[1,128,128]{1,2,0:T(8,128)S(1)} custom-call(f32[1,128,128]{2,1,0:T(8,128)S(1)} %get-tuple-element.62), custom_call_target="InvertDiagBlocksLowerTriangular" | custom-call | tf_op jit(solution)/shard_map/jit(cholesky)/cholesky | solution.py:13
  262.9 11.7 %cholesky.147 = f32[128,128]{1,0:T(8,128)S(1)} custom-call(f32[128,128]{1,0:T(8,128)S(1)} %convolution_subtract_fusion.4), custom_call_target="Cholesky" | custom-call | tf_op jit(solution)/shard_map/jit(cholesky)/cholesky | solution.py:13
  276.7 4.3 while.4
  277.7 1.4 bitcast_dynamic-update-slice_fusion.4
  279.7 1.4 bitcast_dynamic-update-slice_fusion.4
  281.1 19.7 %custom-call.14 = f32[2,128,128]{1,2,0:T(8,128)S(1)} custom-call(f32[2,128,128]{2,1,0:T(8,128)S(1)} %get-tuple-element.21), custom_call_target="InvertDiagBlocksLowerTriangular" | custom-call | tf_op jit(solution)/shard_map/triangular_solve/custom-call.0 | solution.py:15
  301.6 3.8 fusion.6
  306.6 11.7 %cholesky.164 = f32[128,128]{1,0:T(8,128)S(1)} custom-call(f32[128,128]{1,0:T(8,128)S(1)} %cholesky.197), custom_call_target="Cholesky" | custom-call | tf_op jit(solution)/shard_map/jit(cholesky)/cholesky | solution.py:13
  319.0 9.8 %custom-call.15 = f32[1,128,128]{1,2,0:T(8,128)S(1)} custom-call(f32[1,128,128]{2,1,0:T(8,128)S(1)} %get-tuple-element.58), custom_call_target="InvertDiagBlocksLowerTriangular" | custom-call | tf_op jit(solution)/shard_map/jit(cholesky)/cholesky | solution.py:13
  329.4 11.9 %cholesky.181 = f32[128,128]{1,0:T(8,128)S(1)} custom-call(f32[128,128]{1,0:T(8,128)S(1)} %convolution_subtract_fusion.3), custom_call_target="Cholesky" | custom-call | tf_op jit(solution)/shard_map/jit(cholesky)/cholesky | solution.py:13
  343.2 3.9 while.5
  343.9 1.3 bitcast_dynamic-update-slice_fusion.5
  345.8 1.3 bitcast_dynamic-update-slice_fusion.5
  347.2 19.7 %custom-call.16 = f32[2,128,128]{1,2,0:T(8,128)S(1)} custom-call(f32[2,128,128]{2,1,0:T(8,128)S(1)} %get-tuple-element.22), custom_call_target="InvertDiagBlocksLowerTriangular" | custom-call | tf_op jit(solution)/shard_map/triangular_solve/custom-call.0 | solution.py:15
  367.8 2.0 fusion.14
  369.8 2.2 compare_select_fusion
  372.0 4.2 select_bitcast_fusion.1
  376.3 2.9 copy.21
  379.2 1.8 copy.22
  381.0 120.9 %all-reduce.8.cloned.1.call-done = (f32[8,1,256,512]{2,3,0,1:T(8,128)}, f32[8,1,256,512]{2,3,0,1:T(8,128)}) async-done(((f32[8,1,256,512]{2,3,0,1:T(8,128)}, f32[8,1,256,512]{2,3,0,1:T(8,128)}), (f32[8,1,256,512]{2,3,0,1:T(8,128)}, f32[8,1,256,512]{2,3,0,1:T(8,128)})) %all-reduce.8.cloned.1.call-update) | async-done | bytes 8388624 | tf_op jit(solution)/shard_map/psum | solution.py:9
  501.9 7.6 %pad_maximum_fusion = f32[8,2,256,512]{2,3,0,1:T(8,128)} fusion(f32[8,1,256,512]{2,3,0,1:T(8,128)} %get-tuple-element.39, f32[8,1,256,512]{2,3,0,1:T(8,128)} %get-tuple-element.40), kind=kLoop, calls=%fused_computation.8 | loop fusion | flops 2097152 | bytes 16777216 | tf_op jit(solution)/shard_map/stack | solution.py:76
  509.5 9.1 %copy.23 = f32[8,2,256,512]{3,2,1,0:T(8,128)} copy(f32[8,2,256,512]{2,3,0,1:T(8,128)} %pad_maximum_fusion) | data formatting | bytes 16777216 | tf_op jit(solution)/shard_map/stack | solution.py:76
  518.6 132.4 %fusion.2 = f32[8,256,16,256]{3,1,2,0:T(8,128)} fusion(f32[8,256,16,256]{3,2,1,0:T(8,128)} %param.4, f32[8,256,256]{2,1,0:T(8,128)} %copy.22, f32[8,256,256]{2,1,0:T(8,128)} %copy.21, pred[8]{0:T(512)(128)(4,1)S(1)} %fusion.34, pred[16]{0:T(512)(128)(4,1)S(1)} %get-tuple-element.67, pred[16]{0:T(512)(128)(4,1)S(1)} %get-tuple-element.68, ...), kind=kOutput, calls=%fused_computation.7 | convolution fusion | flops 51574210560 | bytes 83886120 | tf_op jit(solution)/shard_map/dot_general | solution.py:21
  651.0 31.8 %copy.26 = f32[8,256,16,256]{3,2,1,0:T(8,128)} copy(f32[8,256,16,256]{3,1,2,0:T(8,128)} %fusion.2) | data formatting | bytes 67108864 | tf_op jit(solution)/shard_map/jit(_where)/select_n | solution.py:83
  (60 shorter events, 10.8 us)
Async XLA Ops:
  6.5 173.1 %all-reduce.12.cloned.1.call-start = ((), (), s32[]{:S(2)}) async-start(), calls=%async_computation.2 | async-start | bytes 8388608 | tf_op jit(solution)/shard_map/psum | solution.py:9
  21.8 216.9 %all-reduce.10.cloned.1.call-start = ((), (), s32[]{:S(2)}) async-start(), calls=%async_computation.1 | async-start | bytes 2097152 | tf_op jit(solution)/shard_map/psum | solution.py:9
  182.4 319.4 %all-reduce.8.cloned.1.call-start = ((), (), s32[]{:S(2)}) async-start(), calls=%async_computation | async-start | bytes 16777216 | tf_op jit(solution)/shard_map/psum | solution.py:9
  301.6 3.8 copy-start.2
  367.8 2.0 copy-start.1
  372.0 4.2 copy-start
Sparse Core Ops, SparseCore 0:
  21.9 157.7 all-reduce.11
  182.9 55.7 all-reduce.9
  376.4 125.4 all-reduce.7
where the time goes:
time: 699 us; the launch traced here: 690 us
  waiting for transfers between devices  335 us (48%)
  matrix products  144 us (21%)
  other arithmetic  126 us (18%)
  local copies, waits for them, and re-layouts  67.6 us (10%)
  between operations  16.5 us (2%)
    psum x3, waiting for transfers between devices, broadcast(): return lax.psum(jnp.where(mine, x, jnp.zeros_like(x)), axis)  335 us
    dot_general x1, matrix products, outer_update(): jnp.dot(own_panel.reshape(row_cycles * block_width, depth), across.reshap...  132 us
    another operation x13, other arithmetic, invert_factor(): lower_factor = jnp.linalg.cholesky(diagonal)  68.8 us
    another operation x5, other arithmetic, invert_factor(): lax.linalg.triangular_solve(lower_factor, identity, left_side=True, lower...  39.4 us
    select_n x1, local copies, waits for them, and re-layouts, on_device(): result = jnp.where(col_global == 1, second_panel[:, :, None, :], result)  31.8 us
  transfers between devices with their start and end apart: 3, of which 3 were waited for; matrix products, arithmetic and copies ran while one was open for 1% of the time, Pallas kernels for 0%

commit v1 on v0

--- a/solution.py
+++ b/solution.py
@@ -6,7 +6,7 @@
 
 def broadcast(x, axis, root):
     mine = lax.axis_index(axis) == root
-    return lax.psum(jnp.where(mine, x, jnp.zeros_like(x)), axis)
+    return jnp.sum(lax.all_gather(jnp.where(mine, x, jnp.zeros_like(x)), axis), axis=0)
 
 
 def invert_factor(diagonal):

time: 699 us -> 1100 us (1.57)
  waiting for transfers between devices: 335 us -> 655 us
  other arithmetic: 126 us -> 173 us
  local copies, waits for them, and re-layouts: 67.6 us -> 104 us
    all_gather x0 -> x6, waiting for transfers between devices: none -> 654 us  [broadcast(): lax.all_gather(jnp.where(mine, x, jnp.zeros_like(x)), axis)]
    psum x3 -> x0, waiting for transfers between devices: 335 us -> none  [broadcast(): return lax.psum(jnp.where(mine, x, jnp.zeros_like(x)), axis)]
    reduce_sum x0 -> x6, other arithmetic: none -> 47.4 us  [broadcast(): jnp.sum(lax.all_gather(jnp.where(mine, x, jnp.zeros_like(x)), axis), axis=0)]
    unnamed x7 -> x11, local copies, waits for them, and re-layouts: 4.56 us -> 39.3 us
  transfers between devices with their start and end apart: 3 -> 6, of which waited for: 3 -> 6; matrix products, arithmetic and copies ran while one was open for 1% -> 4% of each run, Pallas kernels for 0% -> 0%
where the time goes in v1:
time: 1100 us
  waiting for transfers between devices  655 us (60%)
  other arithmetic  173 us (16%)
  matrix products  146 us (13%)
  local copies, waits for them, and re-layouts  104 us (9%)
  between operations  16.7 us (2%)
    all_gather x6, waiting for transfers between devices, broadcast(): lax.all_gather(jnp.where(mine, x, jnp.zeros_like(x)), axis)  654 us
    dot_general x1, matrix products, outer_update(): jnp.dot(own_panel.reshape(row_cycles * block_width, depth), across.reshap...  133 us
    another operation x13, other arithmetic, invert_factor(): lower_factor = jnp.linalg.cholesky(diagonal)  68.7 us
    reduce_sum x6, other arithmetic, broadcast(): jnp.sum(lax.all_gather(jnp.where(mine, x, jnp.zeros_like(x)), axis), axis=0)  47.4 us
    another operation x5, other arithmetic, invert_factor(): lax.linalg.triangular_solve(lower_factor, identity, left_side=True, lower...  39.9 us
    unnamed x11, local copies, waits for them, and re-layouts  39.3 us
    select_n x1, local copies, waits for them, and re-layouts, on_device(): result = jnp.where(col_global == 1, second_panel[:, :, None, :], result)  31.8 us
  transfers between devices with their start and end apart: 6, of which 6 were waited for; matrix products, arithmetic and copies ran while one was open for 4% of the time, Pallas kernels for 0%

profile of v1, /device:TPU:0, one launch (start us, length us, event | category | flops | bytes accessed | tf_op | source)
XLA Modules:
  0.0 1095.2 jit_solution(489182604695309037)
XLA Ops:
  6.5 28.2 %copy.19 = f32[8,256,16,256]{3,1,2,0:T(8,128)S(1)} copy(f32[8,256,16,256]{3,2,1,0:T(8,128)} %param.4) | data formatting | bytes 67108864 | tf_op args[0]
  38.0 151.7 %all-gather.17.cloned.1.call-done = f32[32,256,1,256]{3,1,2,0:T(8,128)} async-done(((f32[8,256,1,256]{3,1,2,0:T(8,128)}), f32[32,256,1,256]{3,1,2,0:T(8,128)}) %all-gather.17.cloned.1.call-update) | async-done | bytes 8388624 | tf_op jit(solution)/shard_map/all_gather | solution.py:9
  189.7 5.6 reduce_sum.54
  195.2 143.8 %all-gather.19.cloned.1.call-done = f32[32,256,1,256]{3,1,2,0:T(8,128)} async-done(((f32[8,256,1,256]{3,1,2,0:T(8,128)}), f32[32,256,1,256]{3,1,2,0:T(8,128)}) %all-gather.19.cloned.1.call-update) | async-done | bytes 8388624 | tf_op jit(solution)/shard_map/all_gather | solution.py:9
  339.1 4.2 reduce_sum.55
  346.8 33.5 %all-gather.11.cloned.1.call-done = f32[8,256,2,256]{3,1,0,2:T(8,128)} async-done(((f32[1,256,2,256]{3,1,0,2:T(8,128)}), f32[8,256,2,256]{3,1,0,2:T(8,128)}) %all-gather.11.cloned.1.call-update) | async-done | bytes 4194320 | tf_op jit(solution)/shard_map/all_gather | solution.py:9
  383.0 35.7 %all-gather.9.cloned.1.call-done = f32[8,256,2,256]{3,1,0,2:T(8,128)} async-done(((f32[1,256,2,256]{3,1,0,2:T(8,128)}), f32[8,256,2,256]{3,1,0,2:T(8,128)}) %all-gather.9.cloned.1.call-update) | async-done | bytes 4194320 | tf_op jit(solution)/shard_map/all_gather | solution.py:9
  421.4 11.7 %cholesky.130 = f32[128,128]{1,0:T(8,128)S(1)} custom-call(f32[128,128]{1,0:T(8,128)S(1)} %cholesky.194), custom_call_target="Cholesky" | custom-call | tf_op jit(solution)/shard_map/jit(cholesky)/cholesky | solution.py:13
  433.2 9.8 custom-call.13
  443.5 11.7 %cholesky.147 = f32[128,128]{1,0:T(8,128)S(1)} custom-call(f32[128,128]{1,0:T(8,128)S(1)} %convolution_subtract_fusion.4), custom_call_target="Cholesky" | custom-call | tf_op jit(solution)/shard_map/jit(cholesky)/cholesky | solution.py:13
  457.2 3.8 while.4
  461.0 20.1 %custom-call.14 = f32[2,128,128]{1,2,0:T(8,128)S(1)} custom-call(f32[2,128,128]{2,1,0:T(8,128)S(1)} %get-tuple-element.21), custom_call_target="InvertDiagBlocksLowerTriangular" | custom-call | tf_op jit(solution)/shard_map/triangular_solve/custom-call.0 | solution.py:15
  482.4 3.7 fusion.6
  486.8 11.7 %cholesky.164 = f32[128,128]{1,0:T(8,128)S(1)} custom-call(f32[128,128]{1,0:T(8,128)S(1)} %cholesky.197), custom_call_target="Cholesky" | custom-call | tf_op jit(solution)/shard_map/jit(cholesky)/cholesky | solution.py:13
  499.2 9.8 custom-call.15
  509.5 11.9 %cholesky.181 = f32[128,128]{1,0:T(8,128)S(1)} custom-call(f32[128,128]{1,0:T(8,128)S(1)} %convolution_subtract_fusion.3), custom_call_target="Cholesky" | custom-call | tf_op jit(solution)/shard_map/jit(cholesky)/cholesky | solution.py:13
  523.4 3.9 while.5
  527.3 19.7 %custom-call.16 = f32[2,128,128]{1,2,0:T(8,128)S(1)} custom-call(f32[2,128,128]{2,1,0:T(8,128)S(1)} %get-tuple-element.22), custom_call_target="InvertDiagBlocksLowerTriangular" | custom-call | tf_op jit(solution)/shard_map/triangular_solve/custom-call.0 | solution.py:15
  547.9 3.5 fusion.14
  553.6 4.2 fusion.3
  557.8 5.3 copy.28
  563.2 5.3 copy.30
  573.7 150.3 %all-gather.13.cloned.1.call-done = f32[8,8,256,512]{3,2,1,0:T(8,128)} async-done(((f32[1,8,256,512]{3,2,1,0:T(8,128)}), f32[8,8,256,512]{3,2,1,0:T(8,128)}) %all-gather.13.cloned.1.call-update) | async-done | bytes 33554448 | tf_op jit(solution)/shard_map/all_gather | solution.py:9
  724.0 17.5 %reduce_sum.58 = f32[8,256,512]{2,1,0:T(8,128)} reduce(f32[8,8,256,512]{3,2,1,0:T(8,128)} %all-gather.13.cloned.1.call-done, f32[]{:T(128)} %constant.83.clone.1), dimensions={0}, to_apply=%region_8.11 | reduce | flops 7340032 | bytes 37748740 | tf_op jit(solution)/shard_map/reduce_sum | solution.py:9
  741.5 5.4 copy.41
  746.9 139.5 %all-gather.15.cloned.1.call-done = f32[8,8,256,512]{3,2,1,0:T(8,128)} async-done(((f32[1,8,256,512]{3,2,1,0:T(8,128)}), f32[8,8,256,512]{3,2,1,0:T(8,128)}) %all-gather.15.cloned.1.call-update) | async-done | bytes 33554448 | tf_op jit(solution)/shard_map/all_gather | solution.py:9
  886.4 15.1 %reduce_sum.59 = f32[8,256,512]{2,1,0:T(8,128)} reduce(f32[8,8,256,512]{3,2,1,0:T(8,128)} %all-gather.15.cloned.1.call-done, f32[]{:T(128)} %constant.83.clone.1), dimensions={0}, to_apply=%region_9.12 | reduce | flops 7340032 | bytes 37748740 | tf_op jit(solution)/shard_map/reduce_sum | solution.py:9
  901.5 5.3 copy.42
  906.8 7.6 pad_maximum_fusion
  914.4 9.1 copy.32
  923.5 132.6 %select_select_fusion = f32[8,256,16,256]{3,1,2,0:T(8,128)} fusion(f32[8,256,256]{2,1,0:T(8,128)} %copy.27, f32[8,256,256]{2,1,0:T(8,128)} %copy.26, pred[8]{0:T(512)(128)(4,1)S(1)} %fusion.34, pred[16]{0:T(512)(128)(4,1)S(1)} %get-tuple-element.61, pred[16]{0:T(512)(128)(4,1)S(1)} %get-tuple-element.62, f32[16,256,512,1]{2,1,0,3:T(8,128)} %bitcast.112, ...), kind=kOutput, calls=%fused_computation.4 | convolution fusion | flops 51574210560 | bytes 83886120 | tf_op jit(solution)/shard_map/dot_general | solution.py:21
  1056.1 31.8 %copy.35 = f32[8,256,16,256]{3,2,1,0:T(8,128)} copy(f32[8,256,16,256]{3,1,2,0:T(8,128)} %select_select_fusion) | data formatting | bytes 67108864 | tf_op jit(solution)/shard_map/jit(_where)/select_n | solution.py:83
  (80 shorter events, 32.9 us)
Async XLA Ops:
  6.5 183.1 %all-gather.17.cloned.1.call-start = ((), (), s32[]{:S(2)}) async-start(), calls=%async_computation.4 | async-start | bytes 10485760 | tf_op jit(solution)/shard_map/all_gather | solution.py:9
  37.2 301.9 %all-gather.19.cloned.1.call-start = ((), (), s32[]{:S(2)}) async-start(), calls=%async_computation.5 | async-start | bytes 10485760 | tf_op jit(solution)/shard_map/all_gather | solution.py:9
  37.9 342.4 %all-gather.11.cloned.1.call-start = ((), (), s32[]{:S(2)}) async-start(), calls=%async_computation.1 | async-start | bytes 4718592 | tf_op jit(solution)/shard_map/all_gather | solution.py:9
  343.3 39.6 %copy-start.1 = (f32[8,256,256]{2,1,0:T(8,128)}, f32[8,256,256]{2,1,0:T(8,128)S(1)}, u32[]{:S(2)}) copy-start(f32[8,256,256]{2,1,0:T(8,128)S(1)} %reduce_sum.55) | copy-start | bytes 6291460
  345.4 73.3 %all-gather.9.cloned.1.call-start = ((), (), s32[]{:S(2)}) async-start(), calls=%async_computation | async-start | bytes 4718592 | tf_op jit(solution)/shard_map/all_gather | solution.py:9
  346.4 377.6 %all-gather.13.cloned.1.call-start = ((), (), s32[]{:S(2)}) async-start(), calls=%async_computation.2 | async-start | bytes 37748736 | tf_op jit(solution)/shard_map/all_gather | solution.py:9
  547.0 4.5 copy-start.2
  553.6 4.2 copy-start
  563.2 323.2 %all-gather.15.cloned.1.call-start = ((), (), s32[]{:S(2)}) async-start(), calls=%async_computation.3 | async-start | bytes 37748736 | tf_op jit(solution)/shard_map/all_gather | solution.py:9
Sparse Core Ops, SparseCore 0:
  37.3 152.3 all-gather.16
  191.2 147.7 all-gather.18
  345.5 34.7 all-gather.10
  382.1 36.5 all-gather.8
  563.3 160.6 all-gather.12
  725.7 160.6 all-gather.14
